TPU v7x, 512 devices: a whole 4x8x8 slice. The times are simulated.
512 devices in a mesh: sx: 32 (over y_lo, z), sy: 16 (over y_hi, x, core).
Axes of the slice: x: 4, y: 8 (y_hi: 2, y_lo: 4; y = y_hi * 4 + y_lo), z: 8, core: 2. Of those that a mesh axis runs over, the one named last changes fastest.
Arguments:
- right_vectors: bfloat16 [32, 1024, 4096], P(None, 'sx', 'sy'), may hold values from -6 to 6
- left_vectors: bfloat16 [64, 1024, 4096], P(None, 'sx', 'sy'), may hold values from -6 to 6
- classes: int32 [1024, 4096], P('sx', 'sy'), may hold values from 0 to 3
- class_energy: float32 [4], replicated, may hold values from -1.5 to 1.5
- bond_mask_grid: int32 [2, 1024, 4096], P(None, 'sx', 'sy'), may hold values 0 or 1
- order: int32 [5], replicated, may hold values from 0 to 4, each once
Outputs:
- gamma: float32 [5, 64, 32], P(None, 'sy')
Inputs may be any that keep to these rules, and one draw needn't show every extreme that they name: Each order from 0 to 4 appears once.
All inputs are finite; a program needn't handle non-finite values. No bound on the sum of `bond_mask_grid` on one device may be relied on, other than what follows from the above.
Results may differ from a plain program's by a relative error of at most 0.0003.
Values sent between devices are 32-bit elements; how exact they have to be, the bound alone decides.
No kernel may reach another device: no remote copies, remote signals or barrier semaphores. Data moves between devices by JAX's collectives and lax.ppermute only.
A program may use at most 64 MiB of HBM per device.

v0:
```python
import jax
import jax.numpy as jnp
from jax import lax
from jax.sharding import PartitionSpec as P

MOMENTS = 5
half_root = 0.8660254037844386
spectral_scale = 4.6


def shifted(value, axis, by):
    length = lax.axis_size(axis)
    return lax.ppermute(value, axis, [(i, (i + by) % length) for i in range(length)])


def with_halo(value, sides, width):
    for axis, dim in sides:
        size, length = (lax.axis_size(axis), value.shape[dim])
        up = [(i, (i + 1) % size) for i in range(size)]
        down = [(j, i) for i, j in up]
        last = lax.slice_in_dim(value, length - width, length, axis=dim)
        initial = lax.slice_in_dim(value, 0, width, axis=dim)
        before = lax.ppermute(last, axis, up)
        after = lax.ppermute(initial, axis, down)
        value = jnp.concatenate([before, value, after], axis=dim)
    return value


def offsets(padded):
    return (padded[:, 2:, 1:-1], padded[:, :-2, 1:-1], padded[:, 1:-1, 2:], padded[:, 1:-1, :-2])


def shards(right_vectors, left_vectors, classes, class_energy, bond_mask_grid, order):
    rows_x, rows_y = classes.shape
    west_row = shifted(bond_mask_grid[0, -1:, :], "sx", 1)
    south_column = shifted(bond_mask_grid[1, :, -1:], "sy", 1)
    hmask = bond_mask_grid[0].astype(jnp.float32)
    vertical_mask = bond_mask_grid[1].astype(jnp.float32)
    west_mask = jnp.concatenate([west_row.astype(jnp.float32), hmask[:-1]], axis=0)
    south_mask = jnp.concatenate([south_column.astype(jnp.float32), vertical_mask[:, :-1]], axis=1)
    xpos = jnp.arange(rows_x, dtype=jnp.int32)[:, None]
    ypos = jnp.arange(rows_y, dtype=jnp.int32)[None, :]
    sublattice_first = ((xpos + ypos) % 2 == 0).astype(jnp.float32)
    sublattice_second = 1.0 - sublattice_first
    sign = sublattice_first - sublattice_second
    upper_neighbour = vertical_mask * sublattice_first
    lower_neighbour = south_mask * sublattice_second
    energy = jnp.zeros((rows_x, rows_y), jnp.float32)
    for level in range(class_energy.shape[0]):
        energy = energy + (classes == level).astype(jnp.float32) * class_energy[level]

    def beside_all(field):
        return offsets(with_halo(field, (("sx", 1), ("sy", 2)), 1))

    nleft = left_vectors.shape[0]
    nright = right_vectors.shape[0]
    cells = rows_x * rows_y
    left_field = left_vectors.astype(jnp.float32)
    left_flat = left_field.reshape(nleft, cells)
    count = MOMENTS
    moments = []
    u_prev = None
    pe, pw, pn, ps = beside_all(right_vectors.astype(jnp.float32))
    u_now = 0.5 * sign * (hmask * pe + west_mask * pw) - upper_neighbour * pn + lower_neighbour * ps
    for step in range(count):
        final = step == count - 1
        parts = None
        parts = beside_all(u_now)
        vel_pe, vel_pw, vel_pn, vel_ps = parts
        moved = (-half_root * (hmask * vel_pe - west_mask * vel_pw)).reshape(nright, cells)
        moments.append(
            jnp.dot(
                left_flat,
                moved.T,
                precision=lax.Precision.HIGHEST,
                preferred_element_type=jnp.float32,
            )
        )
        if not final:
            hamilton_pe, hamilton_pw, hamilton_pn, hamilton_ps = parts
            image = (
                energy * u_now
                - hmask * hamilton_pe
                - west_mask * hamilton_pw
                - upper_neighbour * hamilton_pn
                - lower_neighbour * hamilton_ps
            ) / spectral_scale
            if step == 0:
                u_next = image
            else:
                u_next = 2.0 * image - u_prev
            u_prev, u_now = (u_now, u_next)
    partial_tiles = jnp.stack(moments)
    owned = nleft // lax.axis_size("sy")
    total = lax.psum(partial_tiles, ("sx", "sy"))
    mine = lax.dynamic_slice_in_dim(total, lax.axis_index("sy") * owned, owned, 1)
    all_sites = cells * lax.axis_size("sx") * lax.axis_size("sy")
    mine = mine * (1.0 / jnp.sqrt(jnp.float32(all_sites)))
    select = (order[:, None] == jnp.arange(count, dtype=jnp.int32)[None, :]).astype(jnp.float32)
    return jnp.einsum("sm,mlr->slr", select, mine, precision=lax.Precision.HIGHEST)


def solution(mesh):
    in_specs = (
        P(None, "sx", "sy"),
        P(None, "sx", "sy"),
        P("sx", "sy"),
        P(),
        P(None, "sx", "sy"),
        P(),
    )
    out_specs = P(None, "sy", None)
    return jax.shard_map(shards, mesh=mesh, in_specs=in_specs, out_specs=out_specs, check_vma=False)
```

profile of v0, /device:TPU:1, one launch (start us, length us, event | category | flops | bytes accessed | tf_op | source)
XLA Modules:
  0.0 309.3 jit_solution(4009982580344775790)
XLA Ops:
  1.5 14.5 %collective-permute-start = (f32[32,1,256]{2,0,1:T(8,128)S(1)}, f32[32,1,256]{2,0,1:T(8,128)S(1)}, u32[]{:S(2)}, u32[]{:S(2)}) collective-permute-start(f32[32,1,256]{2,0,1:T(8,128)S(1)} %get-tuple-element.30), channel_id=1, source_target_pairs={{16,0},{32,16},{48,32},{64,48},{80,64},{96,80},{112,96},{128,112},... | collective-permute-start | bytes 98312 | tf_op jit(solution)/shard_map/ppermute | solution.py:24
  18.1 4.0 %collective-permute-start.4 = (s32[32,1]{0,1:T(1,128)S(1)}, s32[32,1]{0,1:T(1,128)S(1)}, u32[]{:S(2)}, u32[]{:S(2)}) collective-permute-start(s32[32,1]{0,1:T(1,128)S(1)} %bitcast.60), channel_id=1, source_target_pairs={{0,1},{1,2},{2,3},{3,4},{4,5},{5,6},{6,7},{7,8},{8,9},{9,10},{10,1... | collective-permute-start | bytes 392 | tf_op jit(solution)/shard_map/ppermute | solution.py:13
  24.3 6.3 %collective-permute-done.1 = s32[1,256]{1,0:T(1,128)S(1)} collective-permute-done((s32[1,256]{1,0:T(1,128)S(1)}, s32[1,256]{1,0:T(1,128)S(1)}, u32[]{:S(2)}, u32[]{:S(2)}) %collective-permute-start.1) | collective-permute-done | bytes 1056 | tf_op jit(solution)/shard_map/ppermute | solution.py:13
  31.4 2.8 collective-permute-start.5
  43.3 4.2 %collective-permute-start.6 = (f32[32,1,256]{2,0,1:T(8,128)S(1)}, f32[32,1,256]{2,0,1:T(8,128)S(1)}, u32[]{:S(2)}, u32[]{:S(2)}) collective-permute-start(f32[32,1,256]{2,0,1:T(8,128)S(1)} %get-tuple-element.28), channel_id=1, source_target_pairs={{16,0},{32,16},{48,32},{64,48},{80,64},{96,80},{112,96},{128,112},... | collective-permute-start | bytes 98312 | tf_op jit(solution)/shard_map/ppermute | solution.py:24
  50.1 6.0 %collective-permute-done.7 = f32[32,1,256]{2,0,1:T(8,128)S(1)} collective-permute-done((f32[32,1,256]{2,0,1:T(8,128)S(1)}, f32[32,1,256]{2,0,1:T(8,128)S(1)}, u32[]{:S(2)}, u32[]{:S(2)}) %collective-permute-start.7) | collective-permute-done | bytes 32800 | tf_op jit(solution)/shard_map/ppermute | solution.py:23
  58.8 2.5 collective-permute-start.9
  62.7 10.5 %collective-permute-start.8 = (f32[32,34,1]{1,0,2:T(8,128)S(1)}, f32[32,34,1]{1,0,2:T(8,128)}, u32[]{:S(2)}, u32[]{:S(2)}) collective-permute-start(f32[32,34,1]{1,0,2:T(8,128)S(1)} %copy.129), channel_id=1, source_target_pairs={{1,0},{2,1},{3,2},{4,3},{5,4},{6,5},{7,6},{8,7},{9,8},{10,9},{11,1... | collective-permute-start | bytes 13064 | tf_op jit(solution)/shard_map/ppermute | solution.py:24
  73.2 3.2 %broadcast_multiply_fusion.1 = (f32[32,256]{1,0:T(8,128)}, f32[32,256]{1,0:T(8,128)S(1)}) fusion(f32[]{:T(128)} %bitcast.12, s32[32,256]{1,0:T(8,128)S(1)} %copy-done.25, f32[]{:T(128)} %bitcast.11, f32[]{:T(128)} %bitcast.10, f32[]{:T(128)} %bitcast.9), kind=kLoop, calls=%fused_computation.158 | loop fusion | flops 98304 | bytes 98320 | tf_op jit(solution)/shard_map/mul | solution.py:82
  77.8 2.1 copy.92
  79.9 2.9 broadcast_multiply_fusion
  84.8 3.4 %collective-permute-start.11 = (f32[32,1,256]{2,0,1:T(8,128)S(1)}, f32[32,1,256]{2,0,1:T(8,128)S(1)}, u32[]{:S(2)}, u32[]{:S(2)}) collective-permute-start(f32[32,1,256]{2,0,1:T(8,128)S(1)} %get-tuple-element.25), channel_id=1, source_target_pairs={{0,16},{16,32},{32,48},{48,64},{64,80},{80,96},{96,112},{112,128},... | collective-permute-start | bytes 98312 | tf_op jit(solution)/shard_map/ppermute | solution.py:23
  88.2 5.2 %collective-permute-done.11 = f32[32,1,256]{2,0,1:T(8,128)S(1)} collective-permute-done((f32[32,1,256]{2,0,1:T(8,128)S(1)}, f32[32,1,256]{2,0,1:T(8,128)S(1)}, u32[]{:S(2)}, u32[]{:S(2)}) %collective-permute-start.11) | collective-permute-done | bytes 32800 | tf_op jit(solution)/shard_map/ppermute | solution.py:23
  96.6 10.8 %collective-permute-start.12 = (f32[32,34,1]{1,0,2:T(8,128)S(1)}, f32[32,34,1]{1,0,2:T(8,128)S(1)}, u32[]{:S(2)}, u32[]{:S(2)}) collective-permute-start(f32[32,34,1]{1,0,2:T(8,128)S(1)} %copy.131), channel_id=1, source_target_pairs={{1,0},{2,1},{3,2},{4,3},{5,4},{6,5},{7,6},{8,7},{9,8},{10,9},{11,1... | collective-permute-start | bytes 13064 | tf_op jit(solution)/shard_map/ppermute | solution.py:24
  110.1 5.8 %fusion.32 = f32[32,32,256]{2,0,1:T(8,128)S(1)} fusion(f32[32,34,1]{2,0,1:T(8,128)} %copy.100, f32[32,1,256]{2,0,1:T(8,128)S(1)} %collective-permute-done.10, f32[32,32,256]{2,0,1:T(8,128)} %copy-done.1, f32[32,1,256]{2,0,1:T(8,128)S(1)} %collective-permute-done.11, f32[32,34,1]{2,0,1:T(8,128)} %copy.98, f32[32,32,256]{2,0,1:T(8,128)} %get-tuple-element.8, ...), kind=kLoop, calls=%fused_computation.59 | loop fusion | flops 9175040 | bytes 4539392 | tf_op jit(solution)/shard_map/sub | solution.py:91
  117.8 3.4 %collective-permute-start.15 = (f32[32,1,256]{2,0,1:T(8,128)S(1)}, f32[32,1,256]{2,0,1:T(8,128)S(1)}, u32[]{:S(2)}, u32[]{:S(2)}) collective-permute-start(f32[32,1,256]{2,0,1:T(8,128)S(1)} %get-tuple-element.23), channel_id=1, source_target_pairs={{0,16},{16,32},{32,48},{48,64},{64,80},{80,96},{96,112},{112,128},... | collective-permute-start | bytes 98312 | tf_op jit(solution)/shard_map/ppermute | solution.py:23
  121.2 5.2 %collective-permute-done.15 = f32[32,1,256]{2,0,1:T(8,128)S(1)} collective-permute-done((f32[32,1,256]{2,0,1:T(8,128)S(1)}, f32[32,1,256]{2,0,1:T(8,128)S(1)}, u32[]{:S(2)}, u32[]{:S(2)}) %collective-permute-start.15) | collective-permute-done | bytes 32800 | tf_op jit(solution)/shard_map/ppermute | solution.py:23
  133.7 11.0 %collective-permute-start.16 = (f32[32,34,1]{1,0,2:T(8,128)}, f32[32,34,1]{1,0,2:T(8,128)}, u32[]{:S(2)}, u32[]{:S(2)}) collective-permute-start(f32[32,34,1]{1,0,2:T(8,128)} %copy.133), channel_id=1, source_target_pairs={{1,0},{2,1},{3,2},{4,3},{5,4},{6,5},{7,6},{8,7},{9,8},{10,9},{11,1... | collective-permute-start | bytes 13064 | tf_op jit(solution)/shard_map/ppermute | solution.py:24
  144.7 2.1 fusion.4
  146.8 2.1 copy.106
  151.0 2.4 fusion.24
  155.4 3.4 %collective-permute-start.19 = (f32[32,1,256]{2,0,1:T(8,128)S(1)}, f32[32,1,256]{2,0,1:T(8,128)S(1)}, u32[]{:S(2)}, u32[]{:S(2)}) collective-permute-start(f32[32,1,256]{2,0,1:T(8,128)S(1)} %get-tuple-element.21), channel_id=1, source_target_pairs={{0,16},{16,32},{32,48},{48,64},{64,80},{80,96},{96,112},{112,128},... | collective-permute-start | bytes 98312 | tf_op jit(solution)/shard_map/ppermute | solution.py:23
  158.8 2.2 fusion.3
  161.0 3.0 collective-permute-done.19
  170.0 10.8 %collective-permute-start.20 = (f32[32,34,1]{1,0,2:T(8,128)}, f32[32,34,1]{1,0,2:T(8,128)}, u32[]{:S(2)}, u32[]{:S(2)}) collective-permute-start(f32[32,34,1]{1,0,2:T(8,128)} %copy.135), channel_id=1, source_target_pairs={{1,0},{2,1},{3,2},{4,3},{5,4},{6,5},{7,6},{8,7},{9,8},{10,9},{11,1... | collective-permute-start | bytes 13064 | tf_op jit(solution)/shard_map/ppermute | solution.py:24
  180.8 2.1 fusion.2
  182.9 2.2 copy.112
  185.1 2.1 copy.110
  191.0 7.5 %collective-permute-start.22 = (f32[32,1,256]{2,0,1:T(8,128)S(1)}, f32[32,1,256]{2,0,1:T(8,128)S(1)}, u32[]{:S(2)}, u32[]{:S(2)}) collective-permute-start(f32[32,1,256]{2,0,1:T(8,128)S(1)} %get-tuple-element.19), channel_id=1, source_target_pairs={{16,0},{32,16},{48,32},{64,48},{80,64},{96,80},{112,96},{128,112},... | collective-permute-start | bytes 98312 | tf_op jit(solution)/shard_map/ppermute | solution.py:24
  198.5 2.1 fusion.1
  200.7 2.2 fusion
  202.8 105.7 %psum.7 = f32[5,64,32]{2,1,0:T(8,128)S(1)} all-reduce(f32[5,64,32]{2,1,0:T(8,128)S(1)} %fusion), channel_id=1, replica_groups=mesh['sx'=32,'sy'=16] {'sx','sy'}, use_global_device_ids=true, to_apply=%region_0.1 | all-reduce | flops 10240 | bytes 81920 | tf_op jit(solution)/shard_map/psum | solution.py:95
  (135 shorter events, 55.3 us)
Async XLA Ops:
  0.0 144.7 %copy-start = (bf16[64,32,256]{2,1,0:T(8,128)(2,1)S(1)}, bf16[64,32,256]{2,1,0:T(8,128)(2,1)}, u32[]{:S(2)}) copy-start(bf16[64,32,256]{2,1,0:T(8,128)(2,1)} %param.7) | copy-start | bytes 3145732
  0.0 17.9 %copy-start.7 = (s32[2,32,256]{2,1,0:T(8,128)S(1)}, s32[2,32,256]{2,1,0:T(8,128)}, u32[]{:S(2)}) copy-start(s32[2,32,256]{2,1,0:T(8,128)} %param.10) | copy-start | bytes 196612
  1.5 29.1 %collective-permute-start = (f32[32,1,256]{2,0,1:T(8,128)S(1)}, f32[32,1,256]{2,0,1:T(8,128)S(1)}, u32[]{:S(2)}, u32[]{:S(2)}) collective-permute-start(f32[32,1,256]{2,0,1:T(8,128)S(1)} %get-tuple-element.30), channel_id=1, source_target_pairs={{16,0},{32,16},{48,32},{64,48},{80,64},{96,80},{112,96},{128,112},... | collective-permute-start | bytes 98312 | tf_op jit(solution)/shard_map/ppermute | solution.py:24
  16.0 14.6 %collective-permute-start.2 = (f32[32,1,256]{2,0,1:T(8,128)S(1)}, f32[32,1,256]{2,0,1:T(8,128)S(1)}, u32[]{:S(2)}, u32[]{:S(2)}) collective-permute-start(f32[32,1,256]{2,0,1:T(8,128)S(1)} %get-tuple-element.29), channel_id=1, source_target_pairs={{0,16},{16,32},{32,48},{48,64},{64,80},{80,96},{96,112},{112,128},... | collective-permute-start | bytes 98312 | tf_op jit(solution)/shard_map/ppermute | solution.py:23
  18.1 6.0 %collective-permute-start.4 = (s32[32,1]{0,1:T(1,128)S(1)}, s32[32,1]{0,1:T(1,128)S(1)}, u32[]{:S(2)}, u32[]{:S(2)}) collective-permute-start(s32[32,1]{0,1:T(1,128)S(1)} %bitcast.60), channel_id=1, source_target_pairs={{0,1},{1,2},{2,3},{3,4},{4,5},{5,6},{6,7},{7,8},{8,9},{9,10},{10,1... | collective-permute-start | bytes 392 | tf_op jit(solution)/shard_map/ppermute | solution.py:13
  22.1 8.5 %collective-permute-start.1 = (s32[1,256]{1,0:T(1,128)S(1)}, s32[1,256]{1,0:T(1,128)S(1)}, u32[]{:S(2)}, u32[]{:S(2)}) collective-permute-start(s32[1,256]{1,0:T(1,128)S(1)} %slice_bitcast_fusion.1), channel_id=1, source_target_pairs={{0,16},{16,32},{32,48},{48,64},{64,80},{80,96},{96,112},{112,128},... | collective-permute-start | bytes 3080 | tf_op jit(solution)/shard_map/ppermute | solution.py:13
  31.4 5.1 %collective-permute-start.5 = (f32[32,34,1]{1,0,2:T(8,128)S(1)}, f32[32,34,1]{1,0,2:T(8,128)S(1)}, u32[]{:S(2)}, u32[]{:S(2)}) collective-permute-start(f32[32,34,1]{1,0,2:T(8,128)S(1)} %copy.128), channel_id=1, source_target_pairs={{0,1},{1,2},{2,3},{3,4},{4,5},{5,6},{6,7},{7,8},{8,9},{9,10},{10,1... | collective-permute-start | bytes 13064 | tf_op jit(solution)/shard_map/ppermute | solution.py:23
  34.6 5.3 %collective-permute-start.3 = (f32[32,34,1]{1,0,2:T(8,128)S(1)}, f32[32,34,1]{1,0,2:T(8,128)S(1)}, u32[]{:S(2)}, u32[]{:S(2)}) collective-permute-start(f32[32,34,1]{1,0,2:T(8,128)S(1)} %copy.127), channel_id=1, source_target_pairs={{1,0},{2,1},{3,2},{4,3},{5,4},{6,5},{7,6},{8,7},{9,8},{10,9},{11,1... | collective-permute-start | bytes 13064 | tf_op jit(solution)/shard_map/ppermute | solution.py:24
  43.3 36.6 %copy-start.5 = (f32[32,32,256]{2,0,1:T(8,128)}, f32[32,32,256]{2,0,1:T(8,128)S(1)}, u32[]{:S(2)}) copy-start(f32[32,32,256]{2,0,1:T(8,128)S(1)} %fusion.44) | copy-start | bytes 3145732
  43.3 6.8 %collective-permute-start.6 = (f32[32,1,256]{2,0,1:T(8,128)S(1)}, f32[32,1,256]{2,0,1:T(8,128)S(1)}, u32[]{:S(2)}, u32[]{:S(2)}) collective-permute-start(f32[32,1,256]{2,0,1:T(8,128)S(1)} %get-tuple-element.28), channel_id=1, source_target_pairs={{16,0},{32,16},{48,32},{64,48},{80,64},{96,80},{112,96},{128,112},... | collective-permute-start | bytes 98312 | tf_op jit(solution)/shard_map/ppermute | solution.py:24
  47.5 8.6 %collective-permute-start.7 = (f32[32,1,256]{2,0,1:T(8,128)S(1)}, f32[32,1,256]{2,0,1:T(8,128)S(1)}, u32[]{:S(2)}, u32[]{:S(2)}) collective-permute-start(f32[32,1,256]{2,0,1:T(8,128)S(1)} %get-tuple-element.27), channel_id=1, source_target_pairs={{0,16},{16,32},{32,48},{48,64},{64,80},{80,96},{96,112},{112,128},... | collective-permute-start | bytes 98312 | tf_op jit(solution)/shard_map/ppermute | solution.py:23
  50.1 29.8 %copy-start.8 = (f32[32,1,256]{2,0,1:T(8,128)}, f32[32,1,256]{2,0,1:T(8,128)S(1)}, u32[]{:S(2)}) copy-start(f32[32,1,256]{2,0,1:T(8,128)S(1)} %collective-permute-done.6) | copy-start | bytes 98308
  56.0 23.9 %copy-start.10 = (f32[32,1,256]{2,0,1:T(8,128)}, f32[32,1,256]{2,0,1:T(8,128)S(1)}, u32[]{:S(2)}) copy-start(f32[32,1,256]{2,0,1:T(8,128)S(1)} %collective-permute-done.7) | copy-start | bytes 98308
  58.8 17.7 %collective-permute-start.9 = (f32[32,34,1]{1,0,2:T(8,128)S(1)}, f32[32,34,1]{1,0,2:T(8,128)S(1)}, u32[]{:S(2)}, u32[]{:S(2)}) collective-permute-start(f32[32,34,1]{1,0,2:T(8,128)S(1)} %copy.130), channel_id=1, source_target_pairs={{0,1},{1,2},{2,3},{3,4},{4,5},{5,6},{6,7},{7,8},{8,9},{9,10},{10,1... | collective-permute-start | bytes 13064 | tf_op jit(solution)/shard_map/ppermute | solution.py:23
  62.7 15.1 %collective-permute-start.8 = (f32[32,34,1]{1,0,2:T(8,128)S(1)}, f32[32,34,1]{1,0,2:T(8,128)}, u32[]{:S(2)}, u32[]{:S(2)}) collective-permute-start(f32[32,34,1]{1,0,2:T(8,128)S(1)} %copy.129), channel_id=1, source_target_pairs={{1,0},{2,1},{3,2},{4,3},{5,4},{6,5},{7,6},{8,7},{9,8},{10,9},{11,1... | collective-permute-start | bytes 13064 | tf_op jit(solution)/shard_map/ppermute | solution.py:24
  82.9 5.3 %collective-permute-start.10 = (f32[32,1,256]{2,0,1:T(8,128)S(1)}, f32[32,1,256]{2,0,1:T(8,128)S(1)}, u32[]{:S(2)}, u32[]{:S(2)}) collective-permute-start(f32[32,1,256]{2,0,1:T(8,128)S(1)} %get-tuple-element.26), channel_id=1, source_target_pairs={{16,0},{32,16},{48,32},{64,48},{80,64},{96,80},{112,96},{128,112},... | collective-permute-start | bytes 98312 | tf_op jit(solution)/shard_map/ppermute | solution.py:24
  84.8 8.6 %collective-permute-start.11 = (f32[32,1,256]{2,0,1:T(8,128)S(1)}, f32[32,1,256]{2,0,1:T(8,128)S(1)}, u32[]{:S(2)}, u32[]{:S(2)}) collective-permute-start(f32[32,1,256]{2,0,1:T(8,128)S(1)} %get-tuple-element.25), channel_id=1, source_target_pairs={{0,16},{16,32},{32,48},{48,64},{64,80},{80,96},{96,112},{112,128},... | collective-permute-start | bytes 98312 | tf_op jit(solution)/shard_map/ppermute | solution.py:23
  88.2 21.9 %copy-start.12 = (f32[32,1,256]{2,0,1:T(8,128)}, f32[32,1,256]{2,0,1:T(8,128)S(1)}, u32[]{:S(2)}) copy-start(f32[32,1,256]{2,0,1:T(8,128)S(1)} %collective-permute-done.10) | copy-start | bytes 98308
  93.4 16.7 %copy-start.14 = (f32[32,1,256]{2,0,1:T(8,128)}, f32[32,1,256]{2,0,1:T(8,128)S(1)}, u32[]{:S(2)}) copy-start(f32[32,1,256]{2,0,1:T(8,128)S(1)} %collective-permute-done.11) | copy-start | bytes 98308
  94.1 13.3 %collective-permute-start.13 = (f32[32,34,1]{1,0,2:T(8,128)S(1)}, f32[32,34,1]{1,0,2:T(8,128)S(1)}, u32[]{:S(2)}, u32[]{:S(2)}) collective-permute-start(f32[32,34,1]{1,0,2:T(8,128)S(1)} %copy.132), channel_id=1, source_target_pairs={{0,1},{1,2},{2,3},{3,4},{4,5},{5,6},{6,7},{7,8},{8,9},{9,10},{10,1... | collective-permute-start | bytes 13064 | tf_op jit(solution)/shard_map/ppermute | solution.py:23
  96.6 12.2 %collective-permute-start.12 = (f32[32,34,1]{1,0,2:T(8,128)S(1)}, f32[32,34,1]{1,0,2:T(8,128)S(1)}, u32[]{:S(2)}, u32[]{:S(2)}) collective-permute-start(f32[32,34,1]{1,0,2:T(8,128)S(1)} %copy.131), channel_id=1, source_target_pairs={{1,0},{2,1},{3,2},{4,3},{5,4},{6,5},{7,6},{8,7},{9,8},{10,9},{11,1... | collective-permute-start | bytes 13064 | tf_op jit(solution)/shard_map/ppermute | solution.py:24
  115.9 5.3 %collective-permute-start.14 = (f32[32,1,256]{2,0,1:T(8,128)S(1)}, f32[32,1,256]{2,0,1:T(8,128)S(1)}, u32[]{:S(2)}, u32[]{:S(2)}) collective-permute-start(f32[32,1,256]{2,0,1:T(8,128)S(1)} %get-tuple-element.24), channel_id=1, source_target_pairs={{16,0},{32,16},{48,32},{64,48},{80,64},{96,80},{112,96},{128,112},... | collective-permute-start | bytes 98312 | tf_op jit(solution)/shard_map/ppermute | solution.py:24
  117.8 8.6 %collective-permute-start.15 = (f32[32,1,256]{2,0,1:T(8,128)S(1)}, f32[32,1,256]{2,0,1:T(8,128)S(1)}, u32[]{:S(2)}, u32[]{:S(2)}) collective-permute-start(f32[32,1,256]{2,0,1:T(8,128)S(1)} %get-tuple-element.23), channel_id=1, source_target_pairs={{0,16},{16,32},{32,48},{48,64},{64,80},{80,96},{96,112},{112,128},... | collective-permute-start | bytes 98312 | tf_op jit(solution)/shard_map/ppermute | solution.py:23
  129.7 17.1 %collective-permute-start.17 = (f32[32,34,1]{1,0,2:T(8,128)S(1)}, f32[32,34,1]{1,0,2:T(8,128)}, u32[]{:S(2)}, u32[]{:S(2)}) collective-permute-start(f32[32,34,1]{1,0,2:T(8,128)S(1)} %copy.134), channel_id=1, source_target_pairs={{0,1},{1,2},{2,3},{3,4},{4,5},{5,6},{6,7},{7,8},{8,9},{9,10},{10,1... | collective-permute-start | bytes 13064 | tf_op jit(solution)/shard_map/ppermute | solution.py:23
  133.7 15.3 %collective-permute-start.16 = (f32[32,34,1]{1,0,2:T(8,128)}, f32[32,34,1]{1,0,2:T(8,128)}, u32[]{:S(2)}, u32[]{:S(2)}) collective-permute-start(f32[32,34,1]{1,0,2:T(8,128)} %copy.133), channel_id=1, source_target_pairs={{1,0},{2,1},{3,2},{4,3},{5,4},{6,5},{7,6},{8,7},{9,8},{10,9},{11,1... | collective-permute-start | bytes 13064 | tf_op jit(solution)/shard_map/ppermute | solution.py:24
  153.4 7.5 %collective-permute-start.18 = (f32[32,1,256]{2,0,1:T(8,128)S(1)}, f32[32,1,256]{2,0,1:T(8,128)S(1)}, u32[]{:S(2)}, u32[]{:S(2)}) collective-permute-start(f32[32,1,256]{2,0,1:T(8,128)S(1)} %get-tuple-element.22), channel_id=1, source_target_pairs={{16,0},{32,16},{48,32},{64,48},{80,64},{96,80},{112,96},{128,112},... | collective-permute-start | bytes 98312 | tf_op jit(solution)/shard_map/ppermute | solution.py:24
  155.4 8.6 %collective-permute-start.19 = (f32[32,1,256]{2,0,1:T(8,128)S(1)}, f32[32,1,256]{2,0,1:T(8,128)S(1)}, u32[]{:S(2)}, u32[]{:S(2)}) collective-permute-start(f32[32,1,256]{2,0,1:T(8,128)S(1)} %get-tuple-element.21), channel_id=1, source_target_pairs={{0,16},{16,32},{32,48},{48,64},{64,80},{80,96},{96,112},{112,128},... | collective-permute-start | bytes 98312 | tf_op jit(solution)/shard_map/ppermute | solution.py:23
  167.0 15.9 %collective-permute-start.21 = (f32[32,34,1]{1,0,2:T(8,128)S(1)}, f32[32,34,1]{1,0,2:T(8,128)}, u32[]{:S(2)}, u32[]{:S(2)}) collective-permute-start(f32[32,34,1]{1,0,2:T(8,128)S(1)} %copy.136), channel_id=1, source_target_pairs={{0,1},{1,2},{2,3},{3,4},{4,5},{5,6},{6,7},{7,8},{8,9},{9,10},{10,1... | collective-permute-start | bytes 13064 | tf_op jit(solution)/shard_map/ppermute | solution.py:23
  170.0 15.1 %collective-permute-start.20 = (f32[32,34,1]{1,0,2:T(8,128)}, f32[32,34,1]{1,0,2:T(8,128)}, u32[]{:S(2)}, u32[]{:S(2)}) collective-permute-start(f32[32,34,1]{1,0,2:T(8,128)} %copy.135), channel_id=1, source_target_pairs={{1,0},{2,1},{3,2},{4,3},{5,4},{6,5},{7,6},{8,7},{9,8},{10,9},{11,1... | collective-permute-start | bytes 13064 | tf_op jit(solution)/shard_map/ppermute | solution.py:24
  189.1 11.5 %collective-permute-start.23 = (f32[32,1,256]{2,0,1:T(8,128)S(1)}, f32[32,1,256]{2,0,1:T(8,128)S(1)}, u32[]{:S(2)}, u32[]{:S(2)}) collective-permute-start(f32[32,1,256]{2,0,1:T(8,128)S(1)} %get-tuple-element.20), channel_id=1, source_target_pairs={{0,16},{16,32},{32,48},{48,64},{64,80},{80,96},{96,112},{112,128},... | collective-permute-start | bytes 98312 | tf_op jit(solution)/shard_map/ppermute | solution.py:23
  191.0 9.6 %collective-permute-start.22 = (f32[32,1,256]{2,0,1:T(8,128)S(1)}, f32[32,1,256]{2,0,1:T(8,128)S(1)}, u32[]{:S(2)}, u32[]{:S(2)}) collective-permute-start(f32[32,1,256]{2,0,1:T(8,128)S(1)} %get-tuple-element.19), channel_id=1, source_target_pairs={{16,0},{32,16},{48,32},{64,48},{80,64},{96,80},{112,96},{128,112},... | collective-permute-start | bytes 98312 | tf_op jit(solution)/shard_map/ppermute | solution.py:24
  200.6 107.9 %copy-start.27 = (s32[5]{0:T(128)S(1)}, s32[5]{0:T(128)}, u32[]{:S(2)}) copy-start(s32[5]{0:T(128)} %param.11) | copy-start | bytes 64
  (20 other events, 186.7 us)
where the time goes:
time: 311 us; the launch traced here: 309 us
  starting transfers between devices  110 us (35%)
  blocking collectives  106 us (34%)
  local copies, waits for them, and re-layouts  34.3 us (11%)
  waiting for transfers between devices  27.7 us (9%)
  other arithmetic  20.3 us (7%)
  matrix products  10.8 us (3%)
    psum x1, blocking collectives, shards(): total = lax.psum(partial_tiles, ('sx', 'sy'))  106 us
    ppermute x11, starting transfers between devices, with_halo(): after = lax.ppermute(initial, axis, down)  76.9 us
    ppermute x11, starting transfers between devices, with_halo(): before = lax.ppermute(last, axis, up)  27 us
    ppermute x11, waiting for transfers between devices, with_halo(): before = lax.ppermute(last, axis, up)  19.3 us
    unnamed x66, local copies, waits for them, and re-layouts  11.6 us
    dot_general x5, matrix products, shards(): jnp.dot(left_flat, moved.T, precision=lax.Precision.HIGHEST, preferred_el...  10.6 us
    sub x3, other arithmetic, shards(): u_next = 2.0 * image - u_prev  10.2 us
    ppermute x5, local copies, waits for them, and re-layouts, with_halo(): after = lax.ppermute(initial, axis, down)  8.93 us
  transfers between devices with their start and end apart: 24, of which 6 were waited for; matrix products, arithmetic and copies ran while one was open for 9% of the time, Pallas kernels for 0%

commit v1 on v0

--- a/solution.py
+++ b/solution.py
@@ -92,7 +92,7 @@
             u_prev, u_now = (u_now, u_next)
     partial_tiles = jnp.stack(moments)
     owned = nleft // lax.axis_size("sy")
-    total = lax.psum(partial_tiles, ("sx", "sy"))
+    total = jnp.sum(lax.all_gather(partial_tiles, ("sx", "sy")), axis=0)
     mine = lax.dynamic_slice_in_dim(total, lax.axis_index("sy") * owned, owned, 1)
     all_sites = cells * lax.axis_size("sx") * lax.axis_size("sy")
     mine = mine * (1.0 / jnp.sqrt(jnp.float32(all_sites)))

time: 311 us -> 1090 us (3.50)
  waiting for transfers between devices: 27.7 us -> 883 us
  blocking collectives: 106 us -> 0 us
  other arithmetic: 20.3 us -> 36.2 us
  between operations: 0.72 us -> 13.9 us
    all_gather x0 -> x1, waiting for transfers between devices: none -> 859 us  [shards(): total = jnp.sum(lax.all_gather(partial_tiles, ('sx', 'sy')), axis=0)]
    psum x1 -> x0, blocking collectives: 106 us -> none  [shards(): total = lax.psum(partial_tiles, ('sx', 'sy'))]
    reduce_sum x0 -> x1, other arithmetic: none -> 16.2 us  [shards(): total = jnp.sum(lax.all_gather(partial_tiles, ('sx', 'sy')), axis=0)]
  transfers between devices with their start and end apart: 24 -> 25, of which waited for: 6 -> 9; matrix products, arithmetic and copies ran while one was open for 9% -> 2% of each run, Pallas kernels for 0% -> 0%
where the time goes in v1:
time: 1090 us
  waiting for transfers between devices  883 us (81%)
  starting transfers between devices  109 us (10%)
  other arithmetic  36.2 us (3%)
  local copies, waits for them, and re-layouts  30.5 us (3%)
  between operations  13.9 us (1%)
  matrix products  13.8 us (1%)
    all_gather x1, waiting for transfers between devices, shards(): total = jnp.sum(lax.all_gather(partial_tiles, ('sx', 'sy')), axis=0)  859 us
    ppermute x11, starting transfers between devices, with_halo(): after = lax.ppermute(initial, axis, down)  76.7 us
    ppermute x11, starting transfers between devices, with_halo(): before = lax.ppermute(last, axis, up)  26.6 us
    ppermute x11, waiting for transfers between devices, with_halo(): before = lax.ppermute(last, axis, up)  22.8 us
  transfers between devices with their start and end apart: 25, of which 9 were waited for; matrix products, arithmetic and copies ran while one was open for 2% of the time, Pallas kernels for 0%

profile of v1, /device:TPU:1, one launch (start us, length us, event | category | flops | bytes accessed | tf_op | source)
XLA Modules:
  0.0 1087.1 jit_solution(9626499952514826554)
XLA Ops:
  8.0 14.5 %collective-permute-start = (f32[32,1,256]{2,0,1:T(8,128)S(1)}, f32[32,1,256]{2,0,1:T(8,128)S(1)}, u32[]{:S(2)}, u32[]{:S(2)}) collective-permute-start(f32[32,1,256]{2,0,1:T(8,128)S(1)} %get-tuple-element.30), channel_id=1, source_target_pairs={{16,0},{32,16},{48,32},{64,48},{80,64},{96,80},{112,96},{128,112},... | collective-permute-start | bytes 98312 | tf_op jit(solution)/shard_map/ppermute | solution.py:24
  26.6 4.0 collective-permute-start.4
  33.6 7.7 collective-permute-start.3
  48.4 7.5 collective-permute-start.6
  58.5 6.0 collective-permute-done.7
  67.2 11.1 %collective-permute-start.8 = (f32[32,34,1]{1,0,2:T(8,128)S(1)}, f32[32,34,1]{1,0,2:T(8,128)S(1)}, u32[]{:S(2)}, u32[]{:S(2)}) collective-permute-start(f32[32,34,1]{1,0,2:T(8,128)S(1)} %copy.83), channel_id=1, source_target_pairs={{1,0},{2,1},{3,2},{4,3},{5,4},{6,5},{7,6},{8,7},{9,8},{10,9},{11,1... | collective-permute-start | bytes 13064 | tf_op jit(solution)/shard_map/ppermute | solution.py:24
  81.7 3.2 broadcast_multiply_fusion.1
  86.2 2.1 copy.62
  88.3 2.9 broadcast_multiply_fusion
  93.2 3.4 collective-permute-start.11
  96.5 5.2 collective-permute-done.11
  103.0 7.9 collective-permute-start.12
  117.1 5.7 fusion.32
  124.8 3.4 collective-permute-start.15
  128.1 5.2 collective-permute-done.15
  136.1 11.5 %collective-permute-start.16 = (f32[32,34,1]{1,0,2:T(8,128)S(1)}, f32[32,34,1]{1,0,2:T(8,128)S(1)}, u32[]{:S(2)}, u32[]{:S(2)}) collective-permute-start(f32[32,34,1]{1,0,2:T(8,128)S(1)} %copy.87), channel_id=1, source_target_pairs={{1,0},{2,1},{3,2},{4,3},{5,4},{6,5},{7,6},{8,7},{9,8},{10,9},{11,1... | collective-permute-start | bytes 13064 | tf_op jit(solution)/shard_map/ppermute | solution.py:24
  149.1 2.1 collective-permute-start.17
  151.2 2.7 fusion.4
  155.3 2.1 copy.72
  157.3 2.4 fusion.24
  161.7 3.4 collective-permute-start.19
  165.0 2.8 fusion.3
  167.8 2.4 collective-permute-done.19
  172.8 8.1 collective-permute-start.20
  183.2 2.7 fusion.2
  190.6 2.5 collective-permute-start.22
  193.1 3.0 collective-permute-start.23
  196.1 2.7 fusion.1
  198.8 2.9 collective-permute-done.23
  201.7 2.8 fusion
  204.5 858.5 %all-gather.3.cloned.1.call-done = f32[2560,64,32]{1,2,0:T(8,128)} async-done(((f32[5,64,32]{1,2,0:T(8,128)}), f32[2560,64,32]{1,2,0:T(8,128)}) %all-gather.3.cloned.1.call-update) | async-done | bytes 20971536 | tf_op jit(solution)/shard_map/all_gather | solution.py:95
  1063.0 16.2 %reduce_sum.9 = f32[5,64,32]{1,2,0:T(8,128)S(1)} reduce(f32[512,5,64,32]{2,3,1,0:T(8,128)} %bitcast.60, f32[]{:T(128)} %constant.46.clone.1), dimensions={0}, to_apply=%region_0.1 | reduce | flops 5232640 | bytes 21012484 | tf_op jit(solution)/shard_map/reduce_sum | solution.py:95
  (113 shorter events, 54.9 us)
Async XLA Ops:
  6.5 144.6 %copy-start = (bf16[64,32,256]{2,1,0:T(8,128)(2,1)S(1)}, bf16[64,32,256]{2,1,0:T(8,128)(2,1)}, u32[]{:S(2)}) copy-start(bf16[64,32,256]{2,1,0:T(8,128)(2,1)} %param.7) | copy-start | bytes 3145732
  6.5 17.9 %copy-start.7 = (s32[2,32,256]{2,1,0:T(8,128)S(1)}, s32[2,32,256]{2,1,0:T(8,128)}, u32[]{:S(2)}) copy-start(s32[2,32,256]{2,1,0:T(8,128)} %param.10) | copy-start | bytes 196612
  6.5 1056.5 %all-gather.3.cloned.1.call-start = ((), (), s32[]{:S(2)}) async-start(), calls=%async_computation | async-start | bytes 42024960 | tf_op jit(solution)/shard_map/all_gather | solution.py:95
  8.0 24.8 %collective-permute-start = (f32[32,1,256]{2,0,1:T(8,128)S(1)}, f32[32,1,256]{2,0,1:T(8,128)S(1)}, u32[]{:S(2)}, u32[]{:S(2)}) collective-permute-start(f32[32,1,256]{2,0,1:T(8,128)S(1)} %get-tuple-element.30), channel_id=1, source_target_pairs={{16,0},{32,16},{48,32},{64,48},{80,64},{96,80},{112,96},{128,112},... | collective-permute-start | bytes 98312 | tf_op jit(solution)/shard_map/ppermute | solution.py:24
  22.5 10.3 collective-permute-start.2
  24.5 8.3 collective-permute-start.1
  26.6 4.7 collective-permute-start.4
  33.6 10.1 collective-permute-start.3
  41.7 3.3 collective-permute-start.5
  48.4 39.9 %copy-start.5 = (f32[32,32,256]{2,0,1:T(8,128)}, f32[32,32,256]{2,0,1:T(8,128)S(1)}, u32[]{:S(2)}) copy-start(f32[32,32,256]{2,0,1:T(8,128)S(1)} %fusion.44) | copy-start | bytes 3145732
  48.4 10.2 collective-permute-start.6
  55.9 8.6 collective-permute-start.7
  65.8 15.9 %copy-start.12 = (s32[32,256]{1,0:T(8,128)S(1)}, s32[32,256]{1,0:T(8,128)}, u32[]{:S(2)}) copy-start(s32[32,256]{1,0:T(8,128)} %param.8) | copy-start | bytes 98308
  67.2 17.7 %collective-permute-start.8 = (f32[32,34,1]{1,0,2:T(8,128)S(1)}, f32[32,34,1]{1,0,2:T(8,128)S(1)}, u32[]{:S(2)}, u32[]{:S(2)}) collective-permute-start(f32[32,34,1]{1,0,2:T(8,128)S(1)} %copy.83), channel_id=1, source_target_pairs={{1,0},{2,1},{3,2},{4,3},{5,4},{6,5},{7,6},{8,7},{9,8},{10,9},{11,1... | collective-permute-start | bytes 13064 | tf_op jit(solution)/shard_map/ppermute | solution.py:24
  79.7 6.5 collective-permute-start.9
  91.2 5.3 collective-permute-start.10
  93.2 8.6 collective-permute-start.11
  103.0 14.2 %copy-start.11 = (f32[32,1,256]{2,0,1:T(8,128)S(1)}, f32[32,1,256]{2,0,1:T(8,128)}, u32[]{:S(2)}) copy-start(f32[32,1,256]{2,0,1:T(8,128)} %copy-done.10) | copy-start | bytes 98308
  103.0 10.2 collective-permute-start.12
  111.3 4.5 collective-permute-start.13
  122.8 5.3 collective-permute-start.14
  124.8 8.6 collective-permute-start.15
  134.6 16.6 %copy-start.6 = (f32[32,32,256]{2,0,1:T(8,128)S(1)}, f32[32,32,256]{2,0,1:T(8,128)}, u32[]{:S(2)}) copy-start(f32[32,32,256]{2,0,1:T(8,128)} %copy-done.5) | copy-start | bytes 3145732
  136.1 17.8 %collective-permute-start.16 = (f32[32,34,1]{1,0,2:T(8,128)S(1)}, f32[32,34,1]{1,0,2:T(8,128)S(1)}, u32[]{:S(2)}, u32[]{:S(2)}) collective-permute-start(f32[32,34,1]{1,0,2:T(8,128)S(1)} %copy.87), channel_id=1, source_target_pairs={{1,0},{2,1},{3,2},{4,3},{5,4},{6,5},{7,6},{8,7},{9,8},{10,9},{11,1... | collective-permute-start | bytes 13064 | tf_op jit(solution)/shard_map/ppermute | solution.py:24
  149.1 6.2 collective-permute-start.17
  159.7 8.1 collective-permute-start.18
  161.7 8.6 collective-permute-start.19
  172.8 13.1 %collective-permute-start.20 = (f32[32,34,1]{1,0,2:T(8,128)S(1)}, f32[32,34,1]{1,0,2:T(8,128)S(1)}, u32[]{:S(2)}, u32[]{:S(2)}) collective-permute-start(f32[32,34,1]{1,0,2:T(8,128)S(1)} %copy.89), channel_id=1, source_target_pairs={{1,0},{2,1},{3,2},{4,3},{5,4},{6,5},{7,6},{8,7},{9,8},{10,9},{11,1... | collective-permute-start | bytes 13064 | tf_op jit(solution)/shard_map/ppermute | solution.py:24
  181.3 6.0 collective-permute-start.21
  190.6 8.2 collective-permute-start.22
  193.1 8.6 collective-permute-start.23
  1063.0 16.4 %copy-start.14 = (s32[5]{0:T(128)S(1)}, s32[5]{0:T(128)}, u32[]{:S(2)}) copy-start(s32[5]{0:T(128)} %param.11) | copy-start | bytes 64
  (8 other events, 63.1 us)
Sparse Core Ops, SparseCore 0:
  204.6 858.3 all-gather.2
